TPU v7x, 32 devices: a whole 2x2x4 slice. The times are simulated.
32 devices in a mesh: depth: 4 (over y, core), image: 8 (over z, x).
Axes of the slice: x: 2, y: 2, z: 4, core: 2. Of those that a mesh axis runs over, the one named last changes fastest.
Arguments:
- populations: float32 [19, 128, 128, 128], P(None, 'depth', 'image'), may hold values from 0 to 0.4, as said below
- transfer: float32 [8, 5, 8], P('image'), may hold values from 0.1 to 1
- direction: int32 [8], P('image'), may hold values from 0 to 1
Outputs:
- final_populations: float32 [19, 128, 128, 128], P(None, 'depth', 'image')
- vorticity: bfloat16 [128, 128, 128], P('depth', 'image')
- images: float32 [8, 4, 128, 128], P('image', None, 'depth')
Inputs may be any that keep to these rules, and one draw needn't show every extreme that they name: `populations`: each population is positive, its lattice weight times a density near one with a perturbation by a rough flow of small speed. `direction`: 0 views from the side of small x, 1 from the side of large x.
All inputs are finite; a program needn't handle non-finite values.
Results may differ from a plain program's by a relative error of at most 0.001.
Values may be sent and summed in bfloat16 or wider, within the bound.
A program may use at most 128 MiB of HBM per device.

v0:
```python
import functools
import math

import jax
import jax.numpy as jnp
from jax import lax
from jax.experimental import pallas as pl
from jax.experimental.pallas import tpu as pltpu
from jax.sharding import PartitionSpec as P

STEPS = 4
MESH = pl.DeviceIdType.MESH

lattice_velocities = (
    (0, 0, 0),
    (1, 0, 0),
    (-1, 0, 0),
    (0, 1, 0),
    (0, -1, 0),
    (0, 0, 1),
    (0, 0, -1),
    (1, 1, 0),
    (-1, -1, 0),
    (1, -1, 0),
    (-1, 1, 0),
    (1, 0, 1),
    (-1, 0, -1),
    (1, 0, -1),
    (-1, 0, 1),
    (0, 1, 1),
    (0, -1, -1),
    (0, 1, -1),
    (0, -1, 1),
)
relaxation = 1.25
bump_width = 0.15
level_offset = 0.05
LOG2E = math.log2(math.e)
SCALE = math.sqrt(LOG2E) / bump_width

COUNT = len(lattice_velocities)
ORDER = (
    [n for n in range(COUNT) if lattice_velocities[n][0] == 1]
    + [n for n in range(COUNT) if lattice_velocities[n][0] == -1]
    + [n for n in range(COUNT) if lattice_velocities[n][0] == 0]
)
SLOT = {number: place for place, number in enumerate(ORDER)}
UP_Y = [n for n in range(COUNT) if lattice_velocities[n][1] == 1]
DOWN_Y = [n for n in range(COUNT) if lattice_velocities[n][1] == -1]
CROSS = len(UP_Y)
CORNERS = [n for n in range(COUNT) if lattice_velocities[n][0] and lattice_velocities[n][1]]
PAIRS = [(n, n + 1) for n in range(1, COUNT, 2)]
LOW = 8
ROWS = 8


def add_all(values):
    while len(values) > 1:
        paired = [a + b for a, b in zip(values[0::2], values[1::2])]
        values = paired + ([values[-1]] if len(values) % 2 else [])
    return values[0]


def moments(field):
    diffs = {}
    sums = [field[0]]
    for plus, minus in PAIRS:
        sums.append(field[plus] + field[minus])
        diffs[plus] = field[plus] - field[minus]
    momentum = []
    for axis in range(3):
        total = diffs[1 + 2 * axis]
        for plus, _ in PAIRS[3:]:
            factor = lattice_velocities[plus][axis]
            if factor == 1:
                total = total + diffs[plus]
            elif factor == -1:
                total = total - diffs[plus]
        momentum.append(total)
    return add_all(sums), momentum


def collide(field):
    density, momentum = moments(field)
    inverse = 1.0 / density
    square = momentum[0] * momentum[0] + momentum[1] * momentum[1] + momentum[2] * momentum[2]
    even = density - 1.5 * (square * inverse)
    keep = 1.0 - relaxation
    result = [keep * field[0] + (relaxation / 3.0) * even] + [None] * (COUNT - 1)
    parts = {}
    for divisor in (18.0, 36.0):
        parts[divisor] = ((relaxation / divisor) * even, (relaxation * 4.5 / divisor) * inverse)
    for plus, minus in PAIRS:
        project = None
        for axis in range(3):
            factor = lattice_velocities[plus][axis]
            if factor:
                if project is None:
                    project = momentum[axis]
                elif factor == 1:
                    project = project + momentum[axis]
                else:
                    project = project - momentum[axis]
        divisor = 18.0 if plus < 7 else 36.0
        base, curve = parts[divisor]
        symmetric = base + curve * (project * project)
        odd = (3.0 * relaxation / divisor) * project
        result[plus] = keep * field[plus] + (symmetric + odd)
        result[minus] = keep * field[minus] + (symmetric - odd)
    return result


def kernel(
    sizes,
    f_hbm,
    par,
    direct,
    F,
    vort,
    img,
    A,
    B,
    E,
    SY,
    RY,
    SC,
    RC,
    U,
    VS,
    VR,
    L,
    G,
    PC,
    PA,
    PS,
    PR,
    in_sem,
    halo_s,
    halo_r,
    flow_s,
    flow_r,
    pa_s,
    pa_r,
    pr_s,
    pr_r,
):
    nd, ni, X, W, NZ, bumps = sizes
    d = lax.axis_index("depth")
    i = lax.axis_index("image")
    halves = W // ROWS
    ratio = ni // nd
    chunks = 4
    step_x = X // chunks

    loads = [
        pltpu.make_async_copy(
            f_hbm.at[:, pl.ds(c * step_x, step_x)],
            F.at[:, pl.ds(c * step_x, step_x)],
            in_sem.at[c],
        )
        for c in range(chunks)
    ]
    for copy in loads:
        copy.start()

    barrier = pltpu.get_barrier_semaphore()
    everyone = nd * ni
    me = d * ni + i

    def greet(offset, carry):
        other = lax.rem(me + offset, everyone)
        pl.semaphore_signal(
            barrier,
            inc=1,
            device_id={"depth": other // ni, "image": lax.rem(other, ni)},
            device_id_type=MESH,
        )
        return carry

    lax.fori_loop(1, everyone, greet, 0)

    ray = X * nd
    lane = lax.broadcasted_iota(jnp.int32, (8, NZ), 1)
    entries = jnp.full((8, NZ), direct[0].astype(jnp.float32), jnp.float32)
    for k in range(bumps):
        for kind in range(5):
            factor = SCALE if kind == 0 else (LOG2E / ray if kind == 1 else 1.0)
            entries = jnp.where(lane == kind * bumps + k, par[kind, 0, k] * factor, entries)
    gain = pltpu.roll(entries, bumps, 1)
    shift = gain * gain - jnp.log2(entries)
    ratios = entries / gain
    for kind in (3, 4):
        ratios = jnp.where(
            lane < kind * bumps, ratios, entries / pltpu.roll(entries, (kind - 1) * bumps, 1)
        )
    table = jnp.where(lane < 2 * bumps, shift, ratios)
    table = jnp.where(lane < bumps, 2.0 * entries, table)
    PC[i] = jnp.where(lane < 5 * bumps, table, entries)[0:1]

    def to(cx, cy):
        return {"depth": lax.rem(d + cx + nd, nd), "image": lax.rem(i + cy + ni, ni)}

    def remote(src, dst, send, recv, target):
        return pltpu.make_async_remote_copy(
            src_ref=src,
            dst_ref=dst,
            send_sem=send,
            recv_sem=recv,
            device_id=target,
            device_id_type=MESH,
        )

    starts = list(range(1, W - 1 - ROWS, ROWS)) + [W - 1 - ROWS]
    edge_rows = (0, W - 1)
    outward = (DOWN_Y, UP_Y)
    inward = (UP_Y, DOWN_Y)

    def pack(b, x, start, values):
        if start == 1:
            for number in DOWN_Y:
                E[b, 0, SLOT[number], pl.ds(ROWS + x, 1), :] = values[number][0:1]
        if start == W - 1 - ROWS:
            for number in UP_Y:
                E[b, 1, SLOT[number], pl.ds(ROWS + x, 1), :] = values[number][ROWS - 1 : ROWS]

    def streamed(S, x, start):
        field = []
        for number in range(COUNT):
            cx, cy, cz = lattice_velocities[number]
            value = S[SLOT[number], x + 1 - cx, pl.ds(LOW + start - cy, ROWS), :]
            if cz:
                value = pltpu.roll(value, cz % NZ, 1)
            field.append(value)
        return field

    def edge_streamed(b, side, x):
        field = []
        for number in range(COUNT):
            cx, _, cz = lattice_velocities[number]
            rows = slice(ROWS + x - cx, 2 * ROWS + x - cx)
            if number in inward[side]:
                value = RY[b, side, inward[side].index(number), rows, :]
            else:
                value = E[b, side, SLOT[number], rows, :]
            if cz:
                value = pltpu.roll(value, cz % NZ, 1)
            field.append(value)
        return field

    def update(S, D, b, x):
        for start in starts:
            values = collide(streamed(S, x, start))
            for number in range(COUNT):
                D[SLOT[number], x + 1, pl.ds(LOW + start, ROWS), :] = values[number]
            pack(b, x, start, values)

    def put_edges(D, b, side, x, values):
        row = LOW + edge_rows[side]
        for number in range(COUNT):
            cx, cy, _ = lattice_velocities[number]
            value = values[number]
            if number in inward[side]:
                for r in range(ROWS):
                    D[SLOT[number], x + r + 1, row : row + 1, :] = value[r : r + 1]
                continue
            if cy == 0:
                E[b, side, SLOT[number], ROWS + x : 2 * ROWS + x, :] = value
            else:
                SY[side, outward[side].index(number), x : x + ROWS, :] = value
            if cx == 1 and x == X - ROWS:
                D[SLOT[number], X, row : row + 1, :] = value[ROWS - 1 : ROWS]
            if cx == -1 and x == 0:
                D[SLOT[number], 1, row : row + 1, :] = value[0:1]

    inner = pl.ds(LOW, W)

    def exchange(D, turn, columns=None):
        slot = turn % 2
        for k, number in enumerate(CORNERS):
            cx, cy, _ = lattice_velocities[number]
            side = 1 if cy == 1 else 0
            edge = X - 1 if cx == 1 else 0
            SC[k] = SY[side, outward[side].index(number), edge : edge + 1, :]
        copies = []

        def add(src, dst, target):
            k = len(copies)
            copies.append(remote(src, dst, halo_s.at[turn, k], halo_r.at[turn, k], target))
            copies[-1].start()

        body = pl.ds(ROWS, X)
        add(SY.at[1], RY.at[slot, 0, :, body], to(0, 1))
        add(SY.at[0], RY.at[slot, 1, :, body], to(0, -1))
        for k, number in enumerate(CORNERS):
            cx, cy, _ = lattice_velocities[number]
            add(SC.at[k], RC.at[slot, k], to(cx, cy))
        if columns is not None:
            for x in (0, X - 1):
                columns(x, 0)
        add(D.at[pl.ds(0, CROSS), X, inner], D.at[pl.ds(0, CROSS), 0, inner], to(1, 0))
        add(D.at[pl.ds(CROSS, CROSS), 1, inner], D.at[pl.ds(CROSS, CROSS), X + 1, inner], to(-1, 0))
        return copies

    def finish(copies, D, turn):
        slot = turn % 2
        for copy in copies:
            copy.wait()
        for number in range(COUNT):
            cx, cy, _ = lattice_velocities[number]
            if cx == 0:
                continue
            plane, place = (0, ROWS - 1) if cx == 1 else (X + 1, ROWS + X)
            for side in range(2):
                if number in inward[side]:
                    k = CORNERS.index(number)
                    j = inward[side].index(number)
                    RY[slot, side, j, place : place + 1, :] = RC[slot, k]
                else:
                    row = LOW + edge_rows[side] - cy
                    E[slot, side, SLOT[number], place : place + 1, :] = D[
                        SLOT[number], plane, row : row + 1, :
                    ]

    def first(x, carry):
        for h in range(halves):
            field = [F[number, x, pl.ds(ROWS * h, ROWS), :] for number in range(COUNT)]
            values = collide(field)
            for number in range(COUNT):
                A[SLOT[number], x + 1, pl.ds(LOW + ROWS * h, ROWS), :] = values[number]
            for side, edge in ((0, 0), (1, ROWS - 1)):
                if h != (0 if side == 0 else halves - 1):
                    continue
                near = 1 if side == 0 else ROWS - 2
                for number in range(COUNT):
                    if lattice_velocities[number][1] == 0:
                        E[0, side, SLOT[number], pl.ds(ROWS + x, 1), :] = values[number][
                            edge : edge + 1
                        ]
                for j, number in enumerate(outward[side]):
                    SY[side, j, pl.ds(x, 1), :] = values[number][edge : edge + 1]
                    E[0, side, SLOT[number], pl.ds(ROWS + x, 1), :] = values[number][
                        near : near + 1
                    ]
        return carry

    for c in range(chunks):
        loads[c].wait()
        lax.fori_loop(c * step_x, (c + 1) * step_x, first, 0)

    pl.semaphore_wait(barrier, everyone - 1)
    shares = [
        remote(PC.at[i], PC.at[i], pa_s.at[o], pa_r.at[o], to(0, o)) for o in range(1, ni)
    ]
    copies = exchange(A, 0)
    for copy in shares:
        copy.start()

    source, target = A, B
    for turn in range(1, STEPS):

        def middle(x, carry, source=source, target=target, turn=turn):
            update(source, target, turn % 2, x)
            return carry

        lax.fori_loop(1, X - 1, middle, 0)
        finish(copies, source, turn - 1)
        for side in range(2):
            for x in range(0, X, ROWS):
                put_edges(target, turn % 2, side, x, collide(edge_streamed((turn - 1) % 2, side, x)))
        copies = exchange(target, turn, middle)
        source, target = target, source

    def flow_of(field):
        density, momentum = moments(field)
        inverse = 1.0 / density
        return [momentum[axis] * inverse for axis in (1, 2, 0)]

    def last(x, carry):
        for start in starts:
            field = streamed(source, x, start)
            for number in range(COUNT):
                F[number, x, pl.ds(start, ROWS), :] = field[number]
            for place, value in enumerate(flow_of(field)):
                U[place, x + 1, pl.ds(LOW + start, ROWS), :] = value
        return carry

    lax.fori_loop(1, X - 1, last, 0)
    finish(copies, source, STEPS - 1)
    for x in (0, X - 1):
        last(x, 0)
    for side in range(2):
        row = edge_rows[side]
        for x in range(0, X, ROWS):
            field = edge_streamed((STEPS - 1) % 2, side, x)
            flow = flow_of(field)
            for place, value in enumerate(flow):
                for r in range(ROWS):
                    U[place, x + r + 1, LOW + row : LOW + row + 1, :] = value[r : r + 1]
            VS[side, 0, x : x + ROWS, :] = flow[1]
            VS[side, 1, x : x + ROWS, :] = flow[2]
    flows = [
        remote(VS.at[1], VR.at[1], flow_s.at[0], flow_r.at[0], to(0, 1)),
        remote(VS.at[0], VR.at[0], flow_s.at[1], flow_r.at[1], to(0, -1)),
        remote(
            U.at[pl.ds(0, 2), X, inner],
            U.at[pl.ds(0, 2), 0, inner],
            flow_s.at[2],
            flow_r.at[2],
            to(1, 0),
        ),
        remote(
            U.at[pl.ds(0, 2), 1, inner],
            U.at[pl.ds(0, 2), X + 1, inner],
            flow_s.at[3],
            flow_r.at[3],
            to(-1, 0),
        ),
    ]
    for copy in flows:
        copy.start()
    for side in range(2):
        row = edge_rows[side]
        for x in range(0, X, ROWS):
            field = edge_streamed((STEPS - 1) % 2, side, x)
            for number in range(COUNT):
                for r in range(ROWS):
                    F[number, x + r, row : row + 1, :] = field[number][r : r + 1]
    for copy in shares:
        copy.wait()

    def expand(m, carry):
        for block in range(PA.shape[1] // 8):
            line = lax.broadcasted_iota(jnp.int32, (8, NZ), 0) + 8 * block
            chosen = jnp.where(lane == line, jnp.broadcast_to(PC[m], (8, NZ)), 0.0)
            value = jnp.sum(chosen, axis=1, keepdims=True)
            PA[m, pl.ds(8 * block, 8), :] = jnp.broadcast_to(value, (8, NZ))
        return carry

    lax.fori_loop(0, ni, expand, 0, unroll=2)
    for copy in flows:
        copy.wait()

    def flow_rows(x, carry):
        for place, j in ((1, 0), (2, 1)):
            U[place, x + 1, pl.ds(LOW - 1, 1), :] = VR[1, j, pl.ds(x, 1), :]
            U[place, x + 1, pl.ds(LOW + W, 1), :] = VR[0, j, pl.ds(x, 1), :]
        return carry

    lax.fori_loop(0, X, flow_rows, 0)

    def spin(x, carry):
        def across_x(place):
            return (U[place, x + 2, inner, :] - U[place, x, inner, :]) * 0.5

        def across_y(place):
            above = U[place, x + 1, pl.ds(LOW + 1, W), :]
            return (above - U[place, x + 1, pl.ds(LOW - 1, W), :]) * 0.5

        def across_z(place):
            value = U[place, x + 1, inner, :]
            return (pltpu.roll(value, NZ - 1, 1) - pltpu.roll(value, 1, 1)) * 0.5

        spin_x = across_y(1) - across_z(0)
        spin_y = across_z(2) - across_x(1)
        spin_z = across_x(0) - across_y(2)
        size = jnp.sqrt(spin_x * spin_x + spin_y * spin_y + spin_z * spin_z)
        rounded = size.astype(jnp.bfloat16)
        vort[x] = rounded
        value = rounded.astype(jnp.float32)
        level = (value / (value + level_offset)) * SCALE
        L[x] = level
        G[x] = jnp.exp2(-(level * level))
        return carry

    lax.fori_loop(0, X, spin, 0, unroll=2)

    owner = i // ratio
    mine = d * ratio + lax.rem(i, ratio)

    def row(m, r):
        return jnp.broadcast_to(PA[m, pl.ds(r, 1), :], (ROWS, NZ))

    def blend(backward, through, colors, local_through, local_colors):
        fade = jnp.where(backward, local_through, 1.0)
        lit = jnp.where(backward, 1.0, through)
        mixed = [color * fade + lit * local for color, local in zip(colors, local_colors)]
        return through * local_through, mixed

    def piece(o, m):
        return remote(
            PS.at[m],
            PR.at[mine],
            pr_s.at[o],
            pr_r.at[mine],
            {"depth": owner, "image": m},
        )

    def render(o, carry):
        m = lax.rem(i + 1 + o, ni)
        backward = row(m, 5 * bumps) > 0.5

        def along(x, state):
            new = []
            levels = [L[x, pl.ds(ROWS * h, ROWS), :] for h in range(halves)]
            totals = [[None] * 4 for h in range(halves)]
            for k in range(bumps):
                centre = row(m, k)
                shift = row(m, bumps + k)
                gains = [row(m, (1 + j) * bumps + k) for j in range(1, 4)]
                for h in range(halves):
                    bump = jnp.exp2(levels[h] * centre - shift)
                    for j in range(4):
                        term = gains[j - 1] * bump if j else bump
                        totals[h][j] = term if k == 0 else totals[h][j] + term
            for h in range(halves):
                through, colors = state[4 * h], state[4 * h + 1 : 4 * h + 4]
                common = G[x, pl.ds(ROWS * h, ROWS), :]
                optical = totals[h][0] * common
                local = jnp.exp2(-optical)
                alpha = (1.0 - local) * common
                shades = [alpha * total for total in totals[h][1:]]
                through, colors = blend(backward, through, colors, local, shades)
                new += [through] + list(colors)
            return tuple(new)

        zero = jnp.zeros((ROWS, NZ), jnp.float32)
        start = (jnp.ones((ROWS, NZ), jnp.float32), zero, zero, zero) * halves
        state = lax.fori_loop(0, X, along, start, unroll=2)
        for h in range(halves):
            through, colors = state[4 * h], state[4 * h + 1 : 4 * h + 4]
            for j, value in enumerate(list(colors) + [through]):
                PS[m, j, pl.ds(ROWS * h, ROWS), :] = value
        local_target = jnp.logical_and(owner == d, m == i)

        @pl.when(local_target)
        def _():
            PR[mine] = PS[m]

        @pl.when(jnp.logical_not(local_target))
        def _():
            piece(o, m).start()

        return carry

    lax.fori_loop(0, ni, render, 0)

    def sent(o, carry):
        m = lax.rem(i + 1 + o, ni)

        @pl.when(jnp.logical_not(jnp.logical_and(owner == d, m == i)))
        def _():
            piece(o, m).wait_send()

        return carry

    def arrived(slot, carry):
        @pl.when(jnp.logical_not(jnp.logical_and(owner == d, slot == mine)))
        def _():
            remote(
                PS.at[0], PR.at[slot], pr_s.at[0], pr_r.at[slot], {"depth": d, "image": i}
            ).wait_recv()

        return carry

    lax.fori_loop(0, nd * ratio, arrived, 0)
    backward = row(i, 5 * bumps) > 0.5
    for part in range(ratio):
        for h in range(halves):
            rows = pl.ds(ROWS * h, ROWS)
            through = jnp.ones((ROWS, NZ), jnp.float32)
            colors = [jnp.zeros((ROWS, NZ), jnp.float32)] * 3
            for slab in range(nd):
                slot = slab * ratio + part
                local = [PR[slot, j, rows, :] for j in range(4)]
                through, colors = blend(backward, through, colors, local[3], local[:3])
            for j, value in enumerate(colors + [1.0 - through]):
                img[0, j, pl.ds(part * W + ROWS * h, ROWS), :] = value
    lax.fori_loop(0, ni, sent, 0)


def on_device(populations, transfer, direction):
    nd, ni = lax.axis_size("depth"), lax.axis_size("image")
    count, X, W, NZ = populations.shape
    bumps = transfer.shape[2]
    assert transfer.shape[0] == 1 and ni % nd == 0 and W % ROWS == 0 and W >= 2 * ROWS and X % 8 == 0
    sizes = (nd, ni, X, W, NZ, bumps)
    ratio = ni // nd
    padded = W + 2 * ROWS
    f32 = jnp.float32
    table = -(-(5 * bumps + 1) // 8) * 8
    dma = pltpu.SemaphoreType.DMA
    return pl.pallas_call(
        functools.partial(kernel, sizes),
        out_shape=(
            pltpu.VMEM(populations.shape, f32),
            jax.ShapeDtypeStruct((X, W, NZ), jnp.bfloat16),
            jax.ShapeDtypeStruct((1, 4, ratio * W, NZ), f32),
        ),
        in_specs=[
            pl.BlockSpec(memory_space=pl.ANY),
            pl.BlockSpec(memory_space=pltpu.SMEM),
            pl.BlockSpec(memory_space=pltpu.SMEM),
        ],
        out_specs=(
            pl.BlockSpec(memory_space=pltpu.VMEM),
            pl.BlockSpec(memory_space=pltpu.VMEM),
            pl.BlockSpec(memory_space=pltpu.VMEM),
        ),
        scratch_shapes=[
            pltpu.VMEM((COUNT, X + 2, padded, NZ), f32),
            pltpu.VMEM((COUNT, X + 2, padded, NZ), f32),
            pltpu.VMEM((2, 2, COUNT, X + 2 * ROWS, NZ), f32),
            pltpu.VMEM((2, CROSS, X, NZ), f32),
            pltpu.VMEM((2, 2, CROSS, X + 2 * ROWS, NZ), f32),
            pltpu.VMEM((4, 1, NZ), f32),
            pltpu.VMEM((2, 4, 1, NZ), f32),
            pltpu.VMEM((3, X + 2, padded, NZ), f32),
            pltpu.VMEM((2, 2, X, NZ), f32),
            pltpu.VMEM((2, 2, X, NZ), f32),
            pltpu.VMEM((X, W, NZ), f32),
            pltpu.VMEM((X, W, NZ), f32),
            pltpu.VMEM((ni, 1, NZ), f32),
            pltpu.VMEM((ni, table, NZ), f32),
            pltpu.VMEM((ni, 4, W, NZ), f32),
            pltpu.VMEM((nd * ratio, 4, W, NZ), f32),
            dma((4,)),
            dma((STEPS, 8)),
            dma((STEPS, 8)),
            dma((4,)),
            dma((4,)),
            dma((ni,)),
            dma((ni,)),
            dma((ni,)),
            dma((nd * ratio,)),
        ],
        compiler_params=pltpu.CompilerParams(
            collective_id=0, has_side_effects=True, vmem_limit_bytes=56 << 20
        ),
    )(populations, transfer.transpose(1, 0, 2), direction)


def solution(mesh):
    in_specs = (P(None, "depth", "image", None), P("image", None, None), P("image"))
    out_specs = (
        P(None, "depth", "image", None),
        P("depth", "image", None),
        P("image", None, "depth", None),
    )
    return jax.shard_map(
        on_device, mesh=mesh, in_specs=in_specs, out_specs=out_specs, check_vma=False
    )
```

profile of v0, /device:TPU:0, one launch (start us, length us, event | category | flops | bytes accessed | tf_op | source)
XLA Modules:
  0.0 55.0 jit_solution(16458200533668422152)
XLA Ops:
  1.3 50.2 %shard_map.58 = (f32[19,32,16,128]{3,2,1,0:T(8,128)S(1)}, bf16[32,16,128]{2,1,0:T(8,128)(2,1)}, f32[1,4,32,128]{3,2,1,0:T(8,128)}) custom-call(f32[19,32,16,128]{3,2,1,0:T(8,128)} %f_hbm.1, f32[5,1,8]{2,1,0:T(1,128)} %bitcast.1, s32[1]{0:T(128)S(6)} %copy.10.direct), custom_call_target="tpu_custom_call" | custom-call | tf_op jit(solution)/shard_map/pallas_call | solution.py:592
  51.5 0.0 copy-start
  51.5 0.0 copy-start.1
  51.5 2.3 %copy.9 = f32[19,32,16,128]{3,2,1,0:T(8,128)} copy(f32[19,32,16,128]{3,2,1,0:T(8,128)S(1)} %get-tuple-element.3) | data formatting | bytes 9961472
  53.7 0.0 copy-done
  53.7 0.7 %copy.11 = bf16[32,16,128]{2,1,0:T(8,128)(2,1)} copy(bf16[32,16,128]{2,1,0:T(8,128)(2,1)S(1)} %copy-done) | data formatting | bytes 262144
  54.4 0.0 copy-done.1
  54.4 0.6 %copy.12 = f32[1,4,32,128]{3,2,1,0:T(8,128)} copy(f32[1,4,32,128]{3,2,1,0:T(8,128)S(1)} %copy-done.1) | data formatting | bytes 131072
Async XLA Ops:
  51.5 2.3 %copy-start = (bf16[32,16,128]{2,1,0:T(8,128)(2,1)S(1)}, bf16[32,16,128]{2,1,0:T(8,128)(2,1)}, u32[]{:S(2)}) copy-start(bf16[32,16,128]{2,1,0:T(8,128)(2,1)} %get-tuple-element.10) | copy-start | bytes 393220
  51.5 2.9 %copy-start.1 = (f32[1,4,32,128]{3,2,1,0:T(8,128)S(1)}, f32[1,4,32,128]{3,2,1,0:T(8,128)}, u32[]{:S(2)}) copy-start(f32[1,4,32,128]{3,2,1,0:T(8,128)} %get-tuple-element.11) | copy-start | bytes 196612
where the time goes:
time: 55.2 us; the launch traced here: 55 us
  Pallas kernels  50.2 us (91%)
  local copies, waits for them, and re-layouts  3.57 us (6%)
  between operations  1.3 us (2%)
    pallas_call x1, Pallas kernels, on_device(): pl.pallas_call(functools.partial(kernel, sizes), out_shape=(pltpu.VMEM(po...  50.2 us
    unnamed x7, local copies, waits for them, and re-layouts  3.57 us

commit v1 on v0

--- a/solution.py
+++ b/solution.py
@@ -52,6 +52,8 @@
 PAIRS = [(n, n + 1) for n in range(1, COUNT, 2)]
 LOW = 8
 ROWS = 8
+CODED = 16
+STEP = 16384.0
 
 
 def add_all(values):
@@ -110,6 +112,19 @@
     return result
 
 
+def weight_of(number):
+    return 1.0 / (18.0 if number < 7 else 36.0)
+
+
+def encode(value, unit):
+    steps = jnp.round(value * (STEP / unit) - STEP)
+    return jnp.clip(steps, -2.0 * STEP, 2.0 * STEP - 1.0).astype(jnp.int32).astype(jnp.int16)
+
+
+def decode(code, unit):
+    return code.astype(jnp.int32).astype(jnp.float32) * (unit / STEP) + unit
+
+
 def kernel(
     sizes,
     f_hbm,
@@ -123,6 +138,8 @@
     E,
     SY,
     RY,
+    SQ,
+    RQ,
     SC,
     RC,
     U,
@@ -283,17 +300,24 @@
             SC[k] = SY[side, outward[side].index(number), edge : edge + 1, :]
         copies = []
 
-        def add(src, dst, target):
-            k = len(copies)
-            copies.append(remote(src, dst, halo_s.at[turn, k], halo_r.at[turn, k], target))
+        def add(src, dst, target, leave=None, land=None):
+            k = len(copies) + 2
+            leave, land = (k, k) if leave is None else (leave, land)
+            copies.append(remote(src, dst, halo_s.at[turn, leave], halo_r.at[turn, land], target))
             copies[-1].start()
 
-        body = pl.ds(ROWS, X)
-        add(SY.at[1], RY.at[slot, 0, :, body], to(0, 1))
-        add(SY.at[0], RY.at[slot, 1, :, body], to(0, -1))
         for k, number in enumerate(CORNERS):
             cx, cy, _ = lattice_velocities[number]
             add(SC.at[k], RC.at[slot, k], to(cx, cy))
+        for side in range(2):
+            for j, number in enumerate(outward[side]):
+                for x in range(0, X, CODED):
+                    rows = slice(x, x + CODED)
+                    SQ[side, j, rows, :] = encode(SY[side, j, rows, :], weight_of(number))
+        far = lax.rem(i, 2)
+        for side in (far, 1 - far):
+            step = {"depth": d, "image": lax.rem(i + 2 * side - 1 + ni, ni)}
+            add(SQ.at[side], RQ.at[slot, 1 - side], step, side, 1 - side)
         if columns is not None:
             for x in (0, X - 1):
                 columns(x, 0)
@@ -305,6 +329,11 @@
         slot = turn % 2
         for copy in copies:
             copy.wait()
+        for side in range(2):
+            for j, number in enumerate(inward[side]):
+                for x in range(0, X, CODED):
+                    value = decode(RQ[slot, side, j, x : x + CODED, :], weight_of(number))
+                    RY[slot, side, j, ROWS + x : ROWS + x + CODED, :] = value
         for number in range(COUNT):
             cx, cy, _ = lattice_velocities[number]
             if cx == 0:
@@ -498,6 +527,7 @@
     def render(o, carry):
         m = lax.rem(i + 1 + o, ni)
         backward = row(m, 5 * bumps) > 0.5
+        sign = jnp.where(backward, 1.0, -1.0)
 
         def along(x, state):
             new = []
@@ -513,22 +543,23 @@
                         term = gains[j - 1] * bump if j else bump
                         totals[h][j] = term if k == 0 else totals[h][j] + term
             for h in range(halves):
-                through, colors = state[4 * h], state[4 * h + 1 : 4 * h + 4]
+                signed, seen, *colors = state[5 * h : 5 * h + 5]
                 common = G[x, pl.ds(ROWS * h, ROWS), :]
-                optical = totals[h][0] * common
-                local = jnp.exp2(-optical)
-                alpha = (1.0 - local) * common
-                shades = [alpha * total for total in totals[h][1:]]
-                through, colors = blend(backward, through, colors, local, shades)
-                new += [through] + list(colors)
+                signed = signed + totals[h][0] * (common * sign)
+                now = jnp.exp2(signed)
+                weight = (seen - now) * common
+                colors = [color + weight * total for color, total in zip(colors, totals[h][1:])]
+                new += [signed, now, *colors]
             return tuple(new)
 
         zero = jnp.zeros((ROWS, NZ), jnp.float32)
-        start = (jnp.ones((ROWS, NZ), jnp.float32), zero, zero, zero) * halves
+        start = (zero, jnp.ones((ROWS, NZ), jnp.float32), zero, zero, zero) * halves
         state = lax.fori_loop(0, X, along, start, unroll=2)
         for h in range(halves):
-            through, colors = state[4 * h], state[4 * h + 1 : 4 * h + 4]
-            for j, value in enumerate(list(colors) + [through]):
+            signed, seen, *colors = state[5 * h : 5 * h + 5]
+            through = jnp.where(backward, jnp.exp2(-signed), seen)
+            factor = jnp.where(backward, -through, 1.0)
+            for j, value in enumerate([color * factor for color in colors] + [through]):
                 PS[m, j, pl.ds(ROWS * h, ROWS), :] = value
         local_target = jnp.logical_and(owner == d, m == i)
 
@@ -578,23 +609,39 @@
     lax.fori_loop(0, ni, sent, 0)
 
 
+def put_out(pieces, F, vort, img, F_out, vort_out, img_out, sems):
+    step = F.shape[1] // pieces
+    copies = [
+        pltpu.make_async_copy(
+            F.at[:, pl.ds(c * step, step)], F_out.at[:, pl.ds(c * step, step)], sems.at[c]
+        )
+        for c in range(pieces)
+    ]
+    copies.append(pltpu.make_async_copy(vort, vort_out, sems.at[pieces]))
+    copies.append(pltpu.make_async_copy(img, img_out, sems.at[pieces + 1]))
+    for copy in copies:
+        copy.start()
+    for copy in copies:
+        copy.wait()
+
+
 def on_device(populations, transfer, direction):
     nd, ni = lax.axis_size("depth"), lax.axis_size("image")
     count, X, W, NZ = populations.shape
     bumps = transfer.shape[2]
-    assert transfer.shape[0] == 1 and ni % nd == 0 and W % ROWS == 0 and W >= 2 * ROWS and X % 8 == 0
+    assert transfer.shape[0] == 1 and ni % nd == 0 and W % ROWS == 0 and W >= 2 * ROWS and X % CODED == 0
     sizes = (nd, ni, X, W, NZ, bumps)
     ratio = ni // nd
     padded = W + 2 * ROWS
     f32 = jnp.float32
     table = -(-(5 * bumps + 1) // 8) * 8
     dma = pltpu.SemaphoreType.DMA
-    return pl.pallas_call(
+    results = pl.pallas_call(
         functools.partial(kernel, sizes),
         out_shape=(
             pltpu.VMEM(populations.shape, f32),
-            jax.ShapeDtypeStruct((X, W, NZ), jnp.bfloat16),
-            jax.ShapeDtypeStruct((1, 4, ratio * W, NZ), f32),
+            pltpu.VMEM((X, W, NZ), jnp.bfloat16),
+            pltpu.VMEM((1, 4, ratio * W, NZ), f32),
         ),
         in_specs=[
             pl.BlockSpec(memory_space=pl.ANY),
@@ -612,6 +659,8 @@
             pltpu.VMEM((2, 2, COUNT, X + 2 * ROWS, NZ), f32),
             pltpu.VMEM((2, CROSS, X, NZ), f32),
             pltpu.VMEM((2, 2, CROSS, X + 2 * ROWS, NZ), f32),
+            pltpu.VMEM((2, CROSS, X, NZ), jnp.int16),
+            pltpu.VMEM((2, 2, CROSS, X, NZ), jnp.int16),
             pltpu.VMEM((4, 1, NZ), f32),
             pltpu.VMEM((2, 4, 1, NZ), f32),
             pltpu.VMEM((3, X + 2, padded, NZ), f32),
@@ -624,8 +673,8 @@
             pltpu.VMEM((ni, 4, W, NZ), f32),
             pltpu.VMEM((nd * ratio, 4, W, NZ), f32),
             dma((4,)),
-            dma((STEPS, 8)),
-            dma((STEPS, 8)),
+            dma((STEPS, 10)),
+            dma((STEPS, 10)),
             dma((4,)),
             dma((4,)),
             dma((ni,)),
@@ -637,6 +686,15 @@
             collective_id=0, has_side_effects=True, vmem_limit_bytes=56 << 20
         ),
     )(populations, transfer.transpose(1, 0, 2), direction)
+    pieces = 4
+    return pl.pallas_call(
+        functools.partial(put_out, pieces),
+        out_shape=tuple(jax.ShapeDtypeStruct(r.shape, r.dtype) for r in results),
+        in_specs=[pl.BlockSpec(memory_space=pltpu.VMEM)] * 3,
+        out_specs=(pl.BlockSpec(memory_space=pl.ANY),) * 3,
+        scratch_shapes=[dma((pieces + 2,))],
+        compiler_params=pltpu.CompilerParams(vmem_limit_bytes=1 << 20),
+    )(*results)
 
 
 def solution(mesh):

time: 55.2 us -> 48.6 us (0.88)
  local copies, waits for them, and re-layouts: 3.57 us -> 0 us
  Pallas kernels: 50.2 us -> 47.2 us
    pallas_call x1, Pallas kernels: 50.2 us -> 44.8 us  [on_device(): pl.pallas_call(functools.partial(kernel, sizes), out_shape=(pltpu.VMEM(po...]
    unnamed x7 -> x0, local copies, waits for them, and re-layouts: 3.57 us -> none
    pallas_call x0 -> x1, Pallas kernels: none -> 2.36 us  [on_device(): pl.pallas_call(functools.partial(put_out, pieces), out_shape=tuple((jax.S...]
where the time goes in v1:
time: 48.6 us; the launch traced here: 48.4 us
  Pallas kernels  47.2 us (97%)
  between operations  1.28 us (3%)
    pallas_call x1, Pallas kernels, on_device(): pl.pallas_call(functools.partial(kernel, sizes), out_shape=(pltpu.VMEM(po...  44.8 us
    pallas_call x1, Pallas kernels, on_device(): pl.pallas_call(functools.partial(put_out, pieces), out_shape=tuple((jax.S...  2.36 us

profile of v1, /device:TPU:0, one launch (start us, length us, event | category | flops | bytes accessed | tf_op | source)
XLA Modules:
  0.0 48.4 jit_solution(16780859008763182699)
XLA Ops:
  1.3 44.8 %shard_map.58 = (f32[19,32,16,128]{3,2,1,0:T(8,128)S(1)}, bf16[32,16,128]{2,1,0:T(8,128)(2,1)S(1)}, f32[1,4,32,128]{3,2,1,0:T(8,128)S(1)}) custom-call(f32[19,32,16,128]{3,2,1,0:T(8,128)} %f_hbm.1, f32[5,1,8]{2,1,0:T(1,128)} %bitcast.1, s32[1]{0:T(128)S(6)} %copy.6.direct), custom_call_target="tpu_custom_call" | custom-call | tf_op jit(solution)/shard_map/pallas_call | solution.py:639
  46.1 2.4 %shard_map.59 = (f32[19,32,16,128]{3,2,1,0:T(8,128)}, bf16[32,16,128]{2,1,0:T(8,128)(2,1)}, f32[1,4,32,128]{3,2,1,0:T(8,128)}) custom-call(f32[19,32,16,128]{3,2,1,0:T(8,128)S(1)} %get-tuple-element.6.F, bf16[32,16,128]{2,1,0:T(8,128)(2,1)S(1)} %get-tuple-element.7.vort, f32[1,4,32,128]{3,2,1,0:T(8,128)S(1)} %get-tuple-element.8.img), custom_call_target="tpu_custom_call" | custom-call | tf_op jit(solution)/shard_map/pallas_call | solution.py:690

commit v2 on v1

--- a/solution.py
+++ b/solution.py
@@ -54,6 +54,7 @@
 ROWS = 8
 CODED = 16
 STEP = 16384.0
+PART_UNITS = ((32768.0, 5.0 / 6.0), (65536.0, 0.0), (65536.0, 0.0))
 
 
 def add_all(values):
@@ -143,8 +144,12 @@
     SC,
     RC,
     U,
-    VS,
-    VR,
+    PYS,
+    PYR,
+    PXS,
+    PXR,
+    CS,
+    CR,
     L,
     G,
     PC,
@@ -154,8 +159,8 @@
     in_sem,
     halo_s,
     halo_r,
-    flow_s,
-    flow_r,
+    part_s,
+    part_r,
     pa_s,
     pa_r,
     pr_s,
@@ -283,13 +288,203 @@
             if cy == 0:
                 E[b, side, SLOT[number], ROWS + x : 2 * ROWS + x, :] = value
             else:
-                SY[side, outward[side].index(number), x : x + ROWS, :] = value
+                SY[side, outward[side].index(number), ROWS + x : 2 * ROWS + x, :] = value
             if cx == 1 and x == X - ROWS:
                 D[SLOT[number], X, row : row + 1, :] = value[ROWS - 1 : ROWS]
             if cx == -1 and x == 0:
                 D[SLOT[number], 1, row : row + 1, :] = value[0:1]
 
     inner = pl.ds(LOW, W)
+
+    def collect(terms, axes):
+        groups = {}
+        for number, value in terms:
+            velocity = lattice_velocities[number]
+            sums = groups.setdefault(velocity[2], [None] * 3)
+            for place, factor in enumerate([1] + [velocity[axis] for axis in axes]):
+                if factor:
+                    value_now = value if factor == 1 else -value
+                    sums[place] = value_now if sums[place] is None else sums[place] + value_now
+        totals = [None] * 3
+        for cz, sums in groups.items():
+            turned = [v if v is None or cz == 0 else pltpu.roll(v, cz % NZ, 1) for v in sums]
+            if 2 in axes:
+                turned[1 + axes.index(2)] = None if cz == 0 else cz * turned[0]
+            for place in range(3):
+                if turned[place] is not None:
+                    old = totals[place]
+                    totals[place] = turned[place] if old is None else old + turned[place]
+        return totals
+
+    def planes_of(side, number):
+        edge, inside = ((0, 1), (X - 1, X - 2))[side]
+        cx = lattice_velocities[number][0]
+        if cx == 0:
+            return edge
+        return inside if cx == 2 * side - 1 else None
+
+    def fill_rows(D, b):
+        zero = jnp.zeros((1, NZ), jnp.float32)
+        for side in range(2):
+            for number in range(COUNT):
+                plane = planes_of(side, number)
+                if plane is None:
+                    continue
+                cy = lattice_velocities[number][1]
+                if cy:
+                    row = LOW - 1 if cy == 1 else LOW + W
+                    D[SLOT[number], plane + 1, row : row + 1, :] = zero
+                    continue
+                for y, row in enumerate(edge_rows):
+                    value = E[b, y, SLOT[number], ROWS + plane : ROWS + plane + 1, :]
+                    D[SLOT[number], plane + 1, LOW + row : LOW + row + 1, :] = value
+
+    def send_parts(D, b):
+        line = lax.broadcasted_iota(jnp.int32, (CODED, NZ), 0)
+        for k, corner in enumerate(CORNERS):
+            cx, cy, _ = lattice_velocities[corner]
+            side = 1 if cy == 1 else 0
+            edge = ROWS + (X - 1 if cx == 1 else 0)
+            for place, cz in enumerate((0, 1, -1)):
+                number = lattice_velocities.index((cx, 0, cz))
+                upper = E[b, side, SLOT[number], edge : edge + 1, :]
+                number = outward[side].index(lattice_velocities.index((0, cy, cz)))
+                lower = SY[side, number, edge : edge + 1, :]
+                if cz == 0:
+                    upper = upper + E[b, side, SLOT[corner], edge : edge + 1, :]
+                    near = edge - cx
+                    lower = lower + SY[side, outward[side].index(corner), near : near + 1, :]
+                CS[k, 2 * place : 2 * place + 1, :] = upper
+                CS[k, 2 * place + 1 : 2 * place + 2, :] = lower
+        for side in range(2):
+            for x in range(0, X, CODED):
+                terms = []
+                for number in range(COUNT):
+                    if number in inward[side]:
+                        continue
+                    cx = lattice_velocities[number][0]
+                    start = ROWS + x - cx
+                    value = E[b, side, SLOT[number], start : start + CODED, :]
+                    if cx == 1 and x == 0:
+                        value = jnp.where(line == 0, 0.0, value)
+                    if cx == -1 and x == X - CODED:
+                        value = jnp.where(line == CODED - 1, 0.0, value)
+                    terms.append((number, value))
+                for place, value in enumerate(collect(terms, (2, 0))):
+                    unit, centre = PART_UNITS[place]
+                    steps = jnp.clip(jnp.round((value - centre) * unit), -32768.0, 32767.0)
+                    code = steps.astype(jnp.int32).astype(jnp.int16)
+                    PYS[side, place, x : x + CODED, :] = code
+        for side in range(2):
+            for h in range(halves):
+                terms = []
+                for number in range(COUNT):
+                    plane = planes_of(side, number)
+                    if plane is None:
+                        continue
+                    rows = pl.ds(LOW + ROWS * h - lattice_velocities[number][1], ROWS)
+                    terms.append((number, D[SLOT[number], plane + 1, rows, :]))
+                for place, value in enumerate(collect(terms, (1, 2))):
+                    PXS[side, place, ROWS * h : ROWS * h + ROWS, :] = value
+        parts = []
+        for k, corner in enumerate(CORNERS):
+            cx, cy, _ = lattice_velocities[corner]
+            parts.append(remote(CS.at[k], CR.at[k], part_s.at[k], part_r.at[k], to(cx, cy)))
+        far = lax.rem(i, 2)
+        for side in (far, 1 - far):
+            step = {"depth": d, "image": lax.rem(i + 2 * side - 1 + ni, ni)}
+            parts.append(
+                remote(
+                    PYS.at[side], PYR.at[1 - side], part_s.at[4 + side], part_r.at[5 - side], step
+                )
+            )
+        for side in range(2):
+            parts.append(
+                remote(
+                    PXS.at[side],
+                    PXR.at[1 - side],
+                    part_s.at[6 + side],
+                    part_r.at[7 - side],
+                    to(2 * side - 1, 0),
+                )
+            )
+        for part in parts:
+            part.start()
+        return parts
+
+    def ghosts(D, slot):
+        line = lax.broadcasted_iota(jnp.int32, (ROWS, NZ), 0)
+        meet = {}
+        for k, corner in enumerate(CORNERS):
+            after = pltpu.roll(CR[k], 1, 1)
+            before = pltpu.roll(CR[k], NZ - 1, 1)
+            plain = CR[k]
+            for y in range(2):
+                up, down = after[2 + y : 3 + y], before[4 + y : 5 + y]
+                meet[lattice_velocities[corner][:2], y] = (plain[y : y + 1] + up + down, up - down)
+        for y in range(2):
+            for number in outward[y]:
+                cx = lattice_velocities[number][0]
+                if cx:
+                    place, plane = (ROWS - 1, 0) if cx == 1 else (ROWS + X, X + 1)
+                    row = LOW + edge_rows[y]
+                    SY[y, outward[y].index(number), place : place + 1, :] = D[
+                        SLOT[number], plane, row : row + 1, :
+                    ]
+        for k, corner in enumerate(CORNERS):
+            cx, cy, _ = lattice_velocities[corner]
+            y = 0 if cy == 1 else 1
+            plane, place = (X, ROWS + X - 1) if cx == 1 else (1, ROWS)
+            row = LOW - 1 if cy == 1 else LOW + W
+            D[SLOT[corner], plane, row : row + 1, :] = RY[
+                slot, y, inward[y].index(corner), place : place + 1, :
+            ]
+        for side in range(2):
+            from_x = 1 - 2 * side
+            plane = X if side else 1
+            for h in range(halves):
+                terms = []
+                for number in range(COUNT):
+                    if lattice_velocities[number][0] == -from_x:
+                        rows = pl.ds(LOW + ROWS * h - lattice_velocities[number][1], ROWS)
+                        terms.append((number, D[SLOT[number], plane, rows, :]))
+                sums = collect(terms, (1, 2))
+                for place in range(3):
+                    sums[place] = sums[place] + PXR[side, place, ROWS * h : ROWS * h + ROWS, :]
+                for at, from_y, wanted in ((0, 1, 0), (ROWS - 1, -1, halves - 1)):
+                    if h == wanted:
+                        mass, along_z = meet[(from_x, from_y), 1]
+                        for place, more in enumerate((mass, from_y * mass, along_z)):
+                            sums[place] = jnp.where(line == at, sums[place] + more, sums[place])
+                inverse = 1.0 / sums[0]
+                for place in range(2):
+                    U[place, (X + 1) * side, pl.ds(LOW + ROWS * h, ROWS), :] = (
+                        sums[1 + place] * inverse
+                    )
+        for side in range(2):
+            from_y = 1 - 2 * side
+            row = LOW + W if side else LOW - 1
+            for x in range(0, X, ROWS):
+                terms = []
+                for j, number in enumerate(outward[side]):
+                    start = ROWS + x - lattice_velocities[number][0]
+                    terms.append((number, SY[side, j, start : start + ROWS, :]))
+                sums = collect(terms, (2, 0))
+                for place in range(3):
+                    unit, centre = PART_UNITS[place]
+                    code = PYR[side, place, x // CODED * CODED : x // CODED * CODED + CODED, :]
+                    value = code.astype(jnp.int32).astype(jnp.float32) * (1.0 / unit) + centre
+                    sums[place] = sums[place] + value[x % CODED : x % CODED + ROWS]
+                for at, from_x, wanted in ((0, 1, 0), (ROWS - 1, -1, X - ROWS)):
+                    if x == wanted:
+                        mass, along_z = meet[(from_x, from_y), 0]
+                        for place, more in enumerate((mass, along_z, from_x * mass)):
+                            sums[place] = jnp.where(line == at, sums[place] + more, sums[place])
+                inverse = 1.0 / sums[0]
+                for place in range(2):
+                    value = sums[1 + place] * inverse
+                    for r in range(ROWS):
+                        U[1 + place, x + r + 1, row : row + 1, :] = value[r : r + 1]
 
     def exchange(D, turn, columns=None):
         slot = turn % 2
@@ -297,7 +492,7 @@
             cx, cy, _ = lattice_velocities[number]
             side = 1 if cy == 1 else 0
             edge = X - 1 if cx == 1 else 0
-            SC[k] = SY[side, outward[side].index(number), edge : edge + 1, :]
+            SC[k] = SY[side, outward[side].index(number), ROWS + edge : ROWS + edge + 1, :]
         copies = []
 
         def add(src, dst, target, leave=None, land=None):
@@ -312,8 +507,8 @@
         for side in range(2):
             for j, number in enumerate(outward[side]):
                 for x in range(0, X, CODED):
-                    rows = slice(x, x + CODED)
-                    SQ[side, j, rows, :] = encode(SY[side, j, rows, :], weight_of(number))
+                    value = SY[side, j, ROWS + x : ROWS + x + CODED, :]
+                    SQ[side, j, x : x + CODED, :] = encode(value, weight_of(number))
         far = lax.rem(i, 2)
         for side in (far, 1 - far):
             step = {"depth": d, "image": lax.rem(i + 2 * side - 1 + ni, ni)}
@@ -321,8 +516,12 @@
         if columns is not None:
             for x in (0, X - 1):
                 columns(x, 0)
+        if turn == STEPS - 1:
+            fill_rows(D, turn % 2)
         add(D.at[pl.ds(0, CROSS), X, inner], D.at[pl.ds(0, CROSS), 0, inner], to(1, 0))
         add(D.at[pl.ds(CROSS, CROSS), 1, inner], D.at[pl.ds(CROSS, CROSS), X + 1, inner], to(-1, 0))
+        if turn == STEPS - 1:
+            copies += send_parts(D, turn % 2)
         return copies
 
     def finish(copies, D, turn):
@@ -366,7 +565,7 @@
                             edge : edge + 1
                         ]
                 for j, number in enumerate(outward[side]):
-                    SY[side, j, pl.ds(x, 1), :] = values[number][edge : edge + 1]
+                    SY[side, j, pl.ds(ROWS + x, 1), :] = values[number][edge : edge + 1]
                     E[0, side, SLOT[number], pl.ds(ROWS + x, 1), :] = values[number][
                         near : near + 1
                     ]
@@ -413,6 +612,17 @@
                 U[place, x + 1, pl.ds(LOW + start, ROWS), :] = value
         return carry
 
+    def expand(m, carry):
+        for block in range(PA.shape[1] // 8):
+            line = lax.broadcasted_iota(jnp.int32, (8, NZ), 0) + 8 * block
+            chosen = jnp.where(lane == line, jnp.broadcast_to(PC[m], (8, NZ)), 0.0)
+            value = jnp.sum(chosen, axis=1, keepdims=True)
+            PA[m, pl.ds(8 * block, 8), :] = jnp.broadcast_to(value, (8, NZ))
+        return carry
+
+    for copy in shares:
+        copy.wait()
+    lax.fori_loop(0, ni, expand, 0, unroll=2)
     lax.fori_loop(1, X - 1, last, 0)
     finish(copies, source, STEPS - 1)
     for x in (0, X - 1):
@@ -421,61 +631,10 @@
         row = edge_rows[side]
         for x in range(0, X, ROWS):
             field = edge_streamed((STEPS - 1) % 2, side, x)
-            flow = flow_of(field)
-            for place, value in enumerate(flow):
+            for place, value in enumerate(flow_of(field)):
                 for r in range(ROWS):
                     U[place, x + r + 1, LOW + row : LOW + row + 1, :] = value[r : r + 1]
-            VS[side, 0, x : x + ROWS, :] = flow[1]
-            VS[side, 1, x : x + ROWS, :] = flow[2]
-    flows = [
-        remote(VS.at[1], VR.at[1], flow_s.at[0], flow_r.at[0], to(0, 1)),
-        remote(VS.at[0], VR.at[0], flow_s.at[1], flow_r.at[1], to(0, -1)),
-        remote(
-            U.at[pl.ds(0, 2), X, inner],
-            U.at[pl.ds(0, 2), 0, inner],
-            flow_s.at[2],
-            flow_r.at[2],
-            to(1, 0),
-        ),
-        remote(
-            U.at[pl.ds(0, 2), 1, inner],
-            U.at[pl.ds(0, 2), X + 1, inner],
-            flow_s.at[3],
-            flow_r.at[3],
-            to(-1, 0),
-        ),
-    ]
-    for copy in flows:
-        copy.start()
-    for side in range(2):
-        row = edge_rows[side]
-        for x in range(0, X, ROWS):
-            field = edge_streamed((STEPS - 1) % 2, side, x)
-            for number in range(COUNT):
-                for r in range(ROWS):
-                    F[number, x + r, row : row + 1, :] = field[number][r : r + 1]
-    for copy in shares:
-        copy.wait()
-
-    def expand(m, carry):
-        for block in range(PA.shape[1] // 8):
-            line = lax.broadcasted_iota(jnp.int32, (8, NZ), 0) + 8 * block
-            chosen = jnp.where(lane == line, jnp.broadcast_to(PC[m], (8, NZ)), 0.0)
-            value = jnp.sum(chosen, axis=1, keepdims=True)
-            PA[m, pl.ds(8 * block, 8), :] = jnp.broadcast_to(value, (8, NZ))
-        return carry
-
-    lax.fori_loop(0, ni, expand, 0, unroll=2)
-    for copy in flows:
-        copy.wait()
-
-    def flow_rows(x, carry):
-        for place, j in ((1, 0), (2, 1)):
-            U[place, x + 1, pl.ds(LOW - 1, 1), :] = VR[1, j, pl.ds(x, 1), :]
-            U[place, x + 1, pl.ds(LOW + W, 1), :] = VR[0, j, pl.ds(x, 1), :]
-        return carry
-
-    lax.fori_loop(0, X, flow_rows, 0)
+    ghosts(source, (STEPS - 1) % 2)
 
     def spin(x, carry):
         def across_x(place):
@@ -574,6 +733,13 @@
         return carry
 
     lax.fori_loop(0, ni, render, 0)
+    for side in range(2):
+        edge = edge_rows[side]
+        for x in range(0, X, ROWS):
+            field = edge_streamed((STEPS - 1) % 2, side, x)
+            for number in range(COUNT):
+                for r in range(ROWS):
+                    F[number, x + r, edge : edge + 1, :] = field[number][r : r + 1]
 
     def sent(o, carry):
         m = lax.rem(i + 1 + o, ni)
@@ -657,15 +823,19 @@
             pltpu.VMEM((COUNT, X + 2, padded, NZ), f32),
             pltpu.VMEM((COUNT, X + 2, padded, NZ), f32),
             pltpu.VMEM((2, 2, COUNT, X + 2 * ROWS, NZ), f32),
-            pltpu.VMEM((2, CROSS, X, NZ), f32),
+            pltpu.VMEM((2, CROSS, X + 2 * ROWS, NZ), f32),
             pltpu.VMEM((2, 2, CROSS, X + 2 * ROWS, NZ), f32),
             pltpu.VMEM((2, CROSS, X, NZ), jnp.int16),
             pltpu.VMEM((2, 2, CROSS, X, NZ), jnp.int16),
             pltpu.VMEM((4, 1, NZ), f32),
             pltpu.VMEM((2, 4, 1, NZ), f32),
             pltpu.VMEM((3, X + 2, padded, NZ), f32),
-            pltpu.VMEM((2, 2, X, NZ), f32),
-            pltpu.VMEM((2, 2, X, NZ), f32),
+            pltpu.VMEM((2, 3, X, NZ), jnp.int16),
+            pltpu.VMEM((2, 3, X, NZ), jnp.int16),
+            pltpu.VMEM((2, 3, W, NZ), f32),
+            pltpu.VMEM((2, 3, W, NZ), f32),
+            pltpu.VMEM((4, 8, NZ), f32),
+            pltpu.VMEM((4, 8, NZ), f32),
             pltpu.VMEM((X, W, NZ), f32),
             pltpu.VMEM((X, W, NZ), f32),
             pltpu.VMEM((ni, 1, NZ), f32),
@@ -675,8 +845,8 @@
             dma((4,)),
             dma((STEPS, 10)),
             dma((STEPS, 10)),
-            dma((4,)),
-            dma((4,)),
+            dma((8,)),
+            dma((8,)),
             dma((ni,)),
             dma((ni,)),
             dma((ni,)),

time: 48.6 us -> 44.3 us (0.912)
  Pallas kernels: 47.2 us -> 42.9 us
    pallas_call x1, Pallas kernels: 44.8 us -> 40.5 us  [on_device(): pl.pallas_call(functools.partial(kernel, sizes), out_shape=(pltpu.VMEM(po...]
where the time goes in v2:
time: 44.3 us; the launch traced here: 44.2 us
  Pallas kernels  42.9 us (97%)
  between operations  1.28 us (3%)
    pallas_call x1, Pallas kernels, on_device(): pl.pallas_call(functools.partial(kernel, sizes), out_shape=(pltpu.VMEM(po...  40.5 us
    pallas_call x1, Pallas kernels, on_device(): pl.pallas_call(functools.partial(put_out, pieces), out_shape=tuple((jax.S...  2.36 us

profile of v2, /device:TPU:0, one launch (start us, length us, event | category | flops | bytes accessed | tf_op | source)
XLA Modules:
  0.0 44.2 jit_solution(11688267348873407509)
XLA Ops:
  1.3 40.5 %shard_map.58 = (f32[19,32,16,128]{3,2,1,0:T(8,128)S(1)}, bf16[32,16,128]{2,1,0:T(8,128)(2,1)S(1)}, f32[1,4,32,128]{3,2,1,0:T(8,128)S(1)}) custom-call(f32[19,32,16,128]{3,2,1,0:T(8,128)} %f_hbm.1, f32[5,1,8]{2,1,0:T(1,128)} %bitcast.1, s32[1]{0:T(128)S(6)} %copy.6.direct), custom_call_target="tpu_custom_call" | custom-call | tf_op jit(solution)/shard_map/pallas_call | solution.py:805
  41.8 2.4 %shard_map.59 = (f32[19,32,16,128]{3,2,1,0:T(8,128)}, bf16[32,16,128]{2,1,0:T(8,128)(2,1)}, f32[1,4,32,128]{3,2,1,0:T(8,128)}) custom-call(f32[19,32,16,128]{3,2,1,0:T(8,128)S(1)} %get-tuple-element.6.F, bf16[32,16,128]{2,1,0:T(8,128)(2,1)S(1)} %get-tuple-element.7.vort, f32[1,4,32,128]{3,2,1,0:T(8,128)S(1)} %get-tuple-element.8.img), custom_call_target="tpu_custom_call" | custom-call | tf_op jit(solution)/shard_map/pallas_call | solution.py:860

commit v3 on v2

--- a/solution.py
+++ b/solution.py
@@ -54,6 +54,8 @@
 ROWS = 8
 CODED = 16
 STEP = 16384.0
+AHEAD = 4
+PIECE = 65535.0
 PART_UNITS = ((32768.0, 5.0 / 6.0), (65536.0, 0.0), (65536.0, 0.0))
 
 
@@ -129,8 +131,8 @@
 def kernel(
     sizes,
     f_hbm,
-    par,
-    direct,
+    par_hbm,
+    direct_hbm,
     F,
     vort,
     img,
@@ -152,18 +154,17 @@
     CR,
     L,
     G,
+    par,
+    direct,
     PC,
     PA,
     PS,
     PR,
-    in_sem,
-    halo_s,
+    first_s,
+    second_s,
     halo_r,
-    part_s,
     part_r,
-    pa_s,
     pa_r,
-    pr_s,
     pr_r,
 ):
     nd, ni, X, W, NZ, bumps = sizes
@@ -171,18 +172,24 @@
     i = lax.axis_index("image")
     halves = W // ROWS
     ratio = ni // nd
-    chunks = 4
+    chunks = 8
     step_x = X // chunks
 
     loads = [
         pltpu.make_async_copy(
             f_hbm.at[:, pl.ds(c * step_x, step_x)],
             F.at[:, pl.ds(c * step_x, step_x)],
-            in_sem.at[c],
+            first_s.at[c],
         )
         for c in range(chunks)
     ]
-    for copy in loads:
+    for copy in loads[:AHEAD]:
+        copy.start()
+    scalars = [
+        pltpu.make_async_copy(par_hbm, par, second_s.at[0]),
+        pltpu.make_async_copy(direct_hbm, direct, second_s.at[1]),
+    ]
+    for copy in scalars:
         copy.start()
 
     barrier = pltpu.get_barrier_semaphore()
@@ -200,24 +207,6 @@
         return carry
 
     lax.fori_loop(1, everyone, greet, 0)
-
-    ray = X * nd
-    lane = lax.broadcasted_iota(jnp.int32, (8, NZ), 1)
-    entries = jnp.full((8, NZ), direct[0].astype(jnp.float32), jnp.float32)
-    for k in range(bumps):
-        for kind in range(5):
-            factor = SCALE if kind == 0 else (LOG2E / ray if kind == 1 else 1.0)
-            entries = jnp.where(lane == kind * bumps + k, par[kind, 0, k] * factor, entries)
-    gain = pltpu.roll(entries, bumps, 1)
-    shift = gain * gain - jnp.log2(entries)
-    ratios = entries / gain
-    for kind in (3, 4):
-        ratios = jnp.where(
-            lane < kind * bumps, ratios, entries / pltpu.roll(entries, (kind - 1) * bumps, 1)
-        )
-    table = jnp.where(lane < 2 * bumps, shift, ratios)
-    table = jnp.where(lane < bumps, 2.0 * entries, table)
-    PC[i] = jnp.where(lane < 5 * bumps, table, entries)[0:1]
 
     def to(cx, cy):
         return {"depth": lax.rem(d + cx + nd, nd), "image": lax.rem(i + cy + ni, ni)}
@@ -389,13 +378,13 @@
         parts = []
         for k, corner in enumerate(CORNERS):
             cx, cy, _ = lattice_velocities[corner]
-            parts.append(remote(CS.at[k], CR.at[k], part_s.at[k], part_r.at[k], to(cx, cy)))
+            parts.append(remote(CS.at[k], CR.at[k], second_s.at[k], part_r.at[k], to(cx, cy)))
         far = lax.rem(i, 2)
         for side in (far, 1 - far):
             step = {"depth": d, "image": lax.rem(i + 2 * side - 1 + ni, ni)}
             parts.append(
                 remote(
-                    PYS.at[side], PYR.at[1 - side], part_s.at[4 + side], part_r.at[5 - side], step
+                    PYS.at[side], PYR.at[1 - side], second_s.at[4 + side], part_r.at[5 - side], step
                 )
             )
         for side in range(2):
@@ -403,7 +392,7 @@
                 remote(
                     PXS.at[side],
                     PXR.at[1 - side],
-                    part_s.at[6 + side],
+                    second_s.at[6 + side],
                     part_r.at[7 - side],
                     to(2 * side - 1, 0),
                 )
@@ -496,9 +485,9 @@
         copies = []
 
         def add(src, dst, target, leave=None, land=None):
-            k = len(copies) + 2
+            k = len(copies) + (2 if len(copies) < 4 else 0)
             leave, land = (k, k) if leave is None else (leave, land)
-            copies.append(remote(src, dst, halo_s.at[turn, leave], halo_r.at[turn, land], target))
+            copies.append(remote(src, dst, first_s.at[leave], halo_r.at[turn % 2, land], target))
             copies[-1].start()
 
         for k, number in enumerate(CORNERS):
@@ -573,11 +562,33 @@
 
     for c in range(chunks):
         loads[c].wait()
+        if c + AHEAD < chunks:
+            loads[c + AHEAD].start()
         lax.fori_loop(c * step_x, (c + 1) * step_x, first, 0)
+
+    for copy in scalars:
+        copy.wait()
+    ray = X * nd
+    lane = lax.broadcasted_iota(jnp.int32, (8, NZ), 1)
+    entries = jnp.full((8, NZ), direct[0].astype(jnp.float32), jnp.float32)
+    for k in range(bumps):
+        for kind in range(5):
+            factor = SCALE if kind == 0 else (LOG2E / ray if kind == 1 else 1.0)
+            entries = jnp.where(lane == kind * bumps + k, par[kind, 0, k] * factor, entries)
+    gain = pltpu.roll(entries, bumps, 1)
+    shift = gain * gain - jnp.log2(entries)
+    ratios = entries / gain
+    for kind in (3, 4):
+        ratios = jnp.where(
+            lane < kind * bumps, ratios, entries / pltpu.roll(entries, (kind - 1) * bumps, 1)
+        )
+    table = jnp.where(lane < 2 * bumps, shift, ratios)
+    table = jnp.where(lane < bumps, 2.0 * entries, table)
+    PC[i] = jnp.where(lane < 5 * bumps, table, entries)[0:1]
 
     pl.semaphore_wait(barrier, everyone - 1)
     shares = [
-        remote(PC.at[i], PC.at[i], pa_s.at[o], pa_r.at[o], to(0, o)) for o in range(1, ni)
+        remote(PC.at[i], PC.at[i], second_s.at[o], pa_r.at[o], to(0, o)) for o in range(1, ni)
     ]
     copies = exchange(A, 0)
     for copy in shares:
@@ -590,11 +601,14 @@
             update(source, target, turn % 2, x)
             return carry
 
-        lax.fori_loop(1, X - 1, middle, 0)
+        lax.fori_loop(1, X - 1, middle, 0, unroll=2)
         finish(copies, source, turn - 1)
         for side in range(2):
             for x in range(0, X, ROWS):
                 put_edges(target, turn % 2, side, x, collide(edge_streamed((turn - 1) % 2, side, x)))
+        if turn == STEPS - 1:
+            for copy in shares:
+                copy.wait()
         copies = exchange(target, turn, middle)
         source, target = target, source
 
@@ -620,8 +634,6 @@
             PA[m, pl.ds(8 * block, 8), :] = jnp.broadcast_to(value, (8, NZ))
         return carry
 
-    for copy in shares:
-        copy.wait()
     lax.fori_loop(0, ni, expand, 0, unroll=2)
     lax.fori_loop(1, X - 1, last, 0)
     finish(copies, source, STEPS - 1)
@@ -660,7 +672,7 @@
         G[x] = jnp.exp2(-(level * level))
         return carry
 
-    lax.fori_loop(0, X, spin, 0, unroll=2)
+    lax.fori_loop(0, X, spin, 0, unroll=4)
 
     owner = i // ratio
     mine = d * ratio + lax.rem(i, ratio)
@@ -678,7 +690,7 @@
         return remote(
             PS.at[m],
             PR.at[mine],
-            pr_s.at[o],
+            first_s.at[o],
             pr_r.at[mine],
             {"depth": owner, "image": m},
         )
@@ -714,12 +726,17 @@
         zero = jnp.zeros((ROWS, NZ), jnp.float32)
         start = (zero, jnp.ones((ROWS, NZ), jnp.float32), zero, zero, zero) * halves
         state = lax.fori_loop(0, X, along, start, unroll=2)
+        parts = []
         for h in range(halves):
             signed, seen, *colors = state[5 * h : 5 * h + 5]
             through = jnp.where(backward, jnp.exp2(-signed), seen)
             factor = jnp.where(backward, -through, 1.0)
-            for j, value in enumerate([color * factor for color in colors] + [through]):
-                PS[m, j, pl.ds(ROWS * h, ROWS), :] = value
+            parts.append([color * factor for color in colors] + [through])
+        for j in range(4):
+            value = jnp.concatenate([part[j] for part in parts], axis=0)
+            unit = PIECE / (bumps if j < 3 else 1.0)
+            steps = jnp.clip(jnp.round(value * unit - 32768.0), -32768.0, 32767.0)
+            PS[m, j] = steps.astype(jnp.int32).astype(jnp.int16)
         local_target = jnp.logical_and(owner == d, m == i)
 
         @pl.when(local_target)
@@ -754,24 +771,25 @@
         @pl.when(jnp.logical_not(jnp.logical_and(owner == d, slot == mine)))
         def _():
             remote(
-                PS.at[0], PR.at[slot], pr_s.at[0], pr_r.at[slot], {"depth": d, "image": i}
+                PS.at[0], PR.at[slot], first_s.at[0], pr_r.at[slot], {"depth": d, "image": i}
             ).wait_recv()
 
         return carry
 
     lax.fori_loop(0, nd * ratio, arrived, 0)
-    backward = row(i, 5 * bumps) > 0.5
+    backward = jnp.broadcast_to(PA[i, pl.ds(5 * bumps, 1), :], (W, NZ)) > 0.5
     for part in range(ratio):
-        for h in range(halves):
-            rows = pl.ds(ROWS * h, ROWS)
-            through = jnp.ones((ROWS, NZ), jnp.float32)
-            colors = [jnp.zeros((ROWS, NZ), jnp.float32)] * 3
-            for slab in range(nd):
-                slot = slab * ratio + part
-                local = [PR[slot, j, rows, :] for j in range(4)]
-                through, colors = blend(backward, through, colors, local[3], local[:3])
-            for j, value in enumerate(colors + [1.0 - through]):
-                img[0, j, pl.ds(part * W + ROWS * h, ROWS), :] = value
+        through = jnp.ones((W, NZ), jnp.float32)
+        colors = [jnp.zeros((W, NZ), jnp.float32)] * 3
+        for slab in range(nd):
+            local = []
+            for j in range(4):
+                unit = (bumps if j < 3 else 1.0) / PIECE
+                code = PR[slab * ratio + part, j].astype(jnp.int32).astype(jnp.float32)
+                local.append(code * unit + 32768.0 * unit)
+            through, colors = blend(backward, through, colors, local[3], local[:3])
+        for j, value in enumerate(colors + [1.0 - through]):
+            img[0, j, part * W : (part + 1) * W, :] = value
     lax.fori_loop(0, ni, sent, 0)
 
 
@@ -811,8 +829,8 @@
         ),
         in_specs=[
             pl.BlockSpec(memory_space=pl.ANY),
-            pl.BlockSpec(memory_space=pltpu.SMEM),
-            pl.BlockSpec(memory_space=pltpu.SMEM),
+            pl.BlockSpec(memory_space=pl.ANY),
+            pl.BlockSpec(memory_space=pl.ANY),
         ],
         out_specs=(
             pl.BlockSpec(memory_space=pltpu.VMEM),
@@ -838,17 +856,16 @@
             pltpu.VMEM((4, 8, NZ), f32),
             pltpu.VMEM((X, W, NZ), f32),
             pltpu.VMEM((X, W, NZ), f32),
+            pltpu.SMEM((5, 1, bumps), f32),
+            pltpu.SMEM((1,), jnp.int32),
             pltpu.VMEM((ni, 1, NZ), f32),
             pltpu.VMEM((ni, table, NZ), f32),
-            pltpu.VMEM((ni, 4, W, NZ), f32),
-            pltpu.VMEM((nd * ratio, 4, W, NZ), f32),
-            dma((4,)),
-            dma((STEPS, 10)),
-            dma((STEPS, 10)),
+            pltpu.VMEM((ni, 4, W, NZ), jnp.int16),
+            pltpu.VMEM((nd * ratio, 4, W, NZ), jnp.int16),
+            dma((max(8, ni),)),
+            dma((max(8, ni),)),
+            dma((2, 8)),
             dma((8,)),
-            dma((8,)),
-            dma((ni,)),
-            dma((ni,)),
             dma((ni,)),
             dma((nd * ratio,)),
         ],
@@ -856,7 +873,7 @@
             collective_id=0, has_side_effects=True, vmem_limit_bytes=56 << 20
         ),
     )(populations, transfer.transpose(1, 0, 2), direction)
-    pieces = 4
+    pieces = 8
     return pl.pallas_call(
         functools.partial(put_out, pieces),
         out_shape=tuple(jax.ShapeDtypeStruct(r.shape, r.dtype) for r in results),

time: 44.3 us -> 42.1 us (0.950)
  Pallas kernels: 42.9 us -> 40.6 us
    pallas_call x1, Pallas kernels: 40.5 us -> 38.3 us  [on_device(): pl.pallas_call(functools.partial(kernel, sizes), out_shape=(pltpu.VMEM(po...]
where the time goes in v3:
time: 42.1 us; the launch traced here: 41.9 us
  Pallas kernels  40.6 us (96%)
  between operations  1.28 us (3%)
    pallas_call x1, Pallas kernels, on_device(): pl.pallas_call(functools.partial(kernel, sizes), out_shape=(pltpu.VMEM(po...  38.3 us
    pallas_call x1, Pallas kernels, on_device(): pl.pallas_call(functools.partial(put_out, pieces), out_shape=tuple((jax.S...  2.38 us

profile of v3, /device:TPU:0, one launch (start us, length us, event | category | flops | bytes accessed | tf_op | source)
XLA Modules:
  0.0 41.9 jit_solution(10232123845601533870)
XLA Ops:
  1.3 38.3 %shard_map.58 = (f32[19,32,16,128]{3,2,1,0:T(8,128)S(1)}, bf16[32,16,128]{2,1,0:T(8,128)(2,1)S(1)}, f32[1,4,32,128]{3,2,1,0:T(8,128)S(1)}) custom-call(f32[19,32,16,128]{3,2,1,0:T(8,128)} %f_hbm.1, f32[5,1,8]{2,1,0:T(1,128)} %bitcast.1, s32[1]{0:T(128)S(6)} %copy.6.direct_hbm), custom_call_target="tpu_custom_call" | custom-call | tf_op jit(solution)/shard_map/pallas_call | solution.py:823
  39.5 2.4 %shard_map.59 = (f32[19,32,16,128]{3,2,1,0:T(8,128)}, bf16[32,16,128]{2,1,0:T(8,128)(2,1)}, f32[1,4,32,128]{3,2,1,0:T(8,128)}) custom-call(f32[19,32,16,128]{3,2,1,0:T(8,128)S(1)} %get-tuple-element.6.F, bf16[32,16,128]{2,1,0:T(8,128)(2,1)S(1)} %get-tuple-element.7.vort, f32[1,4,32,128]{3,2,1,0:T(8,128)S(1)} %get-tuple-element.8.img), custom_call_target="tpu_custom_call" | custom-call | tf_op jit(solution)/shard_map/pallas_call | solution.py:877

commit v4 on v3

--- a/solution.py
+++ b/solution.py
@@ -140,6 +140,7 @@
     B,
     E,
     SY,
+    EI,
     RY,
     SQ,
     RQ,
@@ -265,23 +266,45 @@
                 D[SLOT[number], x + 1, pl.ds(LOW + start, ROWS), :] = values[number]
             pack(b, x, start, values)
 
-    def put_edges(D, b, side, x, values):
-        row = LOW + edge_rows[side]
-        for number in range(COUNT):
-            cx, cy, _ = lattice_velocities[number]
-            value = values[number]
-            if number in inward[side]:
-                for r in range(ROWS):
-                    D[SLOT[number], x + r + 1, row : row + 1, :] = value[r : r + 1]
-                continue
-            if cy == 0:
-                E[b, side, SLOT[number], ROWS + x : 2 * ROWS + x, :] = value
-            else:
-                SY[side, outward[side].index(number), ROWS + x : 2 * ROWS + x, :] = value
-            if cx == 1 and x == X - ROWS:
-                D[SLOT[number], X, row : row + 1, :] = value[ROWS - 1 : ROWS]
-            if cx == -1 and x == 0:
-                D[SLOT[number], 1, row : row + 1, :] = value[0:1]
+    def mirrored(number):
+        cx, cy, cz = lattice_velocities[number]
+        return lattice_velocities.index((cx, -cy, cz))
+
+    def choose(side, low, high):
+        return low if low == high else low + side * (high - low)
+
+    def slot_of(side, number):
+        return choose(side, SLOT[number], SLOT[mirrored(number)])
+
+    def place_of(side, number):
+        lists = (UP_Y, DOWN_Y) if number in UP_Y else (DOWN_Y, UP_Y)
+        return choose(side, lists[0].index(number), lists[1].index(mirrored(number)))
+
+    def corner_of(side, number):
+        return choose(side, CORNERS.index(number), CORNERS.index(mirrored(number)))
+
+    def edges(old, b, side):
+        for x in (0,):
+            field = []
+            for number in range(COUNT):
+                cx, _, cz = lattice_velocities[number]
+                rows = slice(ROWS + x - cx, ROWS + x - cx + X)
+                if number in UP_Y:
+                    value = RY[old, side, place_of(side, number), rows, :]
+                else:
+                    value = E[old, side, slot_of(side, number), rows, :]
+                if cz:
+                    value = pltpu.roll(value, cz % NZ, 1)
+                field.append(value)
+            values = collide(field)
+            for number in range(COUNT):
+                cy = lattice_velocities[number][1]
+                if cy == 1:
+                    EI[side, place_of(side, number), x : x + X, :] = values[number]
+                elif cy == 0:
+                    E[b, side, SLOT[number], ROWS + x : ROWS + x + X, :] = values[number]
+                else:
+                    SY[side, place_of(side, number), ROWS + x : ROWS + x + X, :] = values[number]
 
     inner = pl.ds(LOW, W)
 
@@ -341,8 +364,8 @@
                 lower = SY[side, number, edge : edge + 1, :]
                 if cz == 0:
                     upper = upper + E[b, side, SLOT[corner], edge : edge + 1, :]
-                    near = edge - cx
-                    lower = lower + SY[side, outward[side].index(corner), near : near + 1, :]
+                    deeper = edge - cx
+                    lower = lower + SY[side, outward[side].index(corner), deeper : deeper + 1, :]
                 CS[k, 2 * place : 2 * place + 1, :] = upper
                 CS[k, 2 * place + 1 : 2 * place + 2, :] = lower
         for side in range(2):
@@ -379,8 +402,7 @@
         for k, corner in enumerate(CORNERS):
             cx, cy, _ = lattice_velocities[corner]
             parts.append(remote(CS.at[k], CR.at[k], second_s.at[k], part_r.at[k], to(cx, cy)))
-        far = lax.rem(i, 2)
-        for side in (far, 1 - far):
+        for side in (far, near):
             step = {"depth": d, "image": lax.rem(i + 2 * side - 1 + ni, ni)}
             parts.append(
                 remote(
@@ -475,68 +497,120 @@
                     for r in range(ROWS):
                         U[1 + place, x + r + 1, row : row + 1, :] = value[r : r + 1]
 
-    def exchange(D, turn, columns=None):
+    def across(cx, side):
+        return {
+            "depth": lax.rem(d + cx + nd, nd),
+            "image": lax.rem(i + 2 * side - 1 + ni, ni),
+        }
+
+    def messages(turn, side):
         slot = turn % 2
-        for k, number in enumerate(CORNERS):
+        found = [
+            remote(
+                SQ.at[side],
+                RQ.at[slot, 1 - side],
+                first_s.at[side],
+                halo_r.at[slot, 1 - side],
+                across(0, side),
+            )
+        ]
+        for number in CORNERS:
             cx, cy, _ = lattice_velocities[number]
-            side = 1 if cy == 1 else 0
-            edge = X - 1 if cx == 1 else 0
-            SC[k] = SY[side, outward[side].index(number), ROWS + edge : ROWS + edge + 1, :]
-        copies = []
-
-        def add(src, dst, target, leave=None, land=None):
-            k = len(copies) + (2 if len(copies) < 4 else 0)
-            leave, land = (k, k) if leave is None else (leave, land)
-            copies.append(remote(src, dst, first_s.at[leave], halo_r.at[turn % 2, land], target))
-            copies[-1].start()
-
-        for k, number in enumerate(CORNERS):
+            if cy == -1:
+                k = corner_of(side, number)
+                found.append(
+                    remote(
+                        SC.at[k],
+                        RC.at[slot, k],
+                        first_s.at[2 + k],
+                        halo_r.at[slot, 2 + k],
+                        across(cx, side),
+                    )
+                )
+        return found
+
+    def planes(D, turn):
+        pairs = ((0, X, 0, 1), (CROSS, 1, X + 1, -1))
+        return [
+            remote(
+                D.at[pl.ds(start, CROSS), plane, inner],
+                D.at[pl.ds(start, CROSS), land, inner],
+                first_s.at[6 + k],
+                halo_r.at[turn % 2, 6 + k],
+                to(cx, 0),
+            )
+            for k, (start, plane, land, cx) in enumerate(pairs)
+        ]
+
+    def send_side(turn, side):
+        for number in CORNERS:
             cx, cy, _ = lattice_velocities[number]
-            add(SC.at[k], RC.at[slot, k], to(cx, cy))
-        for side in range(2):
-            for j, number in enumerate(outward[side]):
-                for x in range(0, X, CODED):
-                    value = SY[side, j, ROWS + x : ROWS + x + CODED, :]
-                    SQ[side, j, x : x + CODED, :] = encode(value, weight_of(number))
-        far = lax.rem(i, 2)
-        for side in (far, 1 - far):
-            step = {"depth": d, "image": lax.rem(i + 2 * side - 1 + ni, ni)}
-            add(SQ.at[side], RQ.at[slot, 1 - side], step, side, 1 - side)
-        if columns is not None:
-            for x in (0, X - 1):
-                columns(x, 0)
-        if turn == STEPS - 1:
-            fill_rows(D, turn % 2)
-        add(D.at[pl.ds(0, CROSS), X, inner], D.at[pl.ds(0, CROSS), 0, inner], to(1, 0))
-        add(D.at[pl.ds(CROSS, CROSS), 1, inner], D.at[pl.ds(CROSS, CROSS), X + 1, inner], to(-1, 0))
-        if turn == STEPS - 1:
-            copies += send_parts(D, turn % 2)
-        return copies
-
-    def finish(copies, D, turn):
+            if cy == -1:
+                edge = ROWS + (X - 1 if cx == 1 else 0)
+                row = SY[side, place_of(side, number), edge : edge + 1, :]
+                SC[corner_of(side, number)] = row
+        copies = messages(turn, side)
+        for copy in copies[1:]:
+            copy.start()
+        for number in DOWN_Y:
+            j = place_of(side, number)
+            for x in range(0, X, CODED):
+                value = SY[side, j, ROWS + x : ROWS + x + CODED, :]
+                SQ[side, j, x : x + CODED, :] = encode(value, weight_of(number))
+        copies[0].start()
+
+    def receive_side(D, turn, side):
         slot = turn % 2
-        for copy in copies:
-            copy.wait()
-        for side in range(2):
-            for j, number in enumerate(inward[side]):
-                for x in range(0, X, CODED):
-                    value = decode(RQ[slot, side, j, x : x + CODED, :], weight_of(number))
-                    RY[slot, side, j, ROWS + x : ROWS + x + CODED, :] = value
+        for copy in messages(turn, side):
+            copy.wait_send()
+        for copy in messages(turn, 1 - side):
+            copy.wait_recv()
+        for number in UP_Y:
+            j = place_of(side, number)
+            for x in range(0, X, CODED):
+                value = decode(RQ[slot, side, j, x : x + CODED, :], weight_of(number))
+                RY[slot, side, j, ROWS + x : ROWS + x + CODED, :] = value
         for number in range(COUNT):
             cx, cy, _ = lattice_velocities[number]
             if cx == 0:
                 continue
             plane, place = (0, ROWS - 1) if cx == 1 else (X + 1, ROWS + X)
+            if cy == 1:
+                j = place_of(side, number)
+                RY[slot, side, j, place : place + 1, :] = RC[slot, corner_of(side, number)]
+            else:
+                row = LOW - cy + side * (W - 1 + 2 * cy)
+                k = slot_of(side, number)
+                E[slot, side, k, place : place + 1, :] = D[k, plane, pl.ds(row, 1), :]
+
+    def inward_rows(D, x):
+        for side in range(2):
+            row = LOW + edge_rows[side]
+            for j, number in enumerate(inward[side]):
+                D[SLOT[number], x + 1, row : row + 1, :] = EI[side, j, pl.ds(x, 1), :]
+
+    def corner_rows(D, b):
+        for x, wanted in ((0, -1), (X - 1, 1)):
+            inward_rows(D, x)
             for side in range(2):
-                if number in inward[side]:
-                    k = CORNERS.index(number)
-                    j = inward[side].index(number)
-                    RY[slot, side, j, place : place + 1, :] = RC[slot, k]
-                else:
-                    row = LOW + edge_rows[side] - cy
-                    E[slot, side, SLOT[number], place : place + 1, :] = D[
-                        SLOT[number], plane, row : row + 1, :
-                    ]
+                row = LOW + edge_rows[side]
+                for number in range(COUNT):
+                    cx, cy, _ = lattice_velocities[number]
+                    if cx != wanted or number in inward[side]:
+                        continue
+                    at = slice(ROWS + x, ROWS + x + 1)
+                    if cy:
+                        value = SY[side, outward[side].index(number), at, :]
+                    else:
+                        value = E[b, side, SLOT[number], at, :]
+                    D[SLOT[number], x + 1, row : row + 1, :] = value
+
+    far = lax.rem(i, 2)
+    near = 1 - far
+    span = max(1, ni // 2)
+    inside = (lax.rem(i + 1, ni) // 2 + span - 1) // span
+    lead = far + inside * (near - far)
+    follow = 1 - lead
 
     def first(x, carry):
         for h in range(halves):
@@ -590,8 +664,9 @@
     shares = [
         remote(PC.at[i], PC.at[i], second_s.at[o], pa_r.at[o], to(0, o)) for o in range(1, ni)
     ]
-    copies = exchange(A, 0)
-    for copy in shares:
+    for side in (far, near):
+        send_side(0, side)
+    for copy in planes(A, 0) + shares:
         copy.start()
 
     source, target = A, B
@@ -602,15 +677,30 @@
             return carry
 
         lax.fori_loop(1, X - 1, middle, 0, unroll=2)
-        finish(copies, source, turn - 1)
-        for side in range(2):
-            for x in range(0, X, ROWS):
-                put_edges(target, turn % 2, side, x, collide(edge_streamed((turn - 1) % 2, side, x)))
+        for copy in planes(source, turn - 1):
+            copy.wait()
+        for side in (lead, follow):
+            receive_side(source, turn - 1, side)
+            edges((turn - 1) % 2, turn % 2, side)
+            send_side(turn, side)
+        for x in (0, X - 1):
+            middle(x, 0)
+        corner_rows(target, turn % 2)
         if turn == STEPS - 1:
-            for copy in shares:
-                copy.wait()
-        copies = exchange(target, turn, middle)
+            fill_rows(target, turn % 2)
+        for copy in planes(target, turn):
+            copy.start()
+
+        def settle(x, carry, target=target):
+            inward_rows(target, x)
+            return carry
+
+        lax.fori_loop(1, X - 1, settle, 0)
         source, target = target, source
+
+    for copy in shares:
+        copy.wait()
+    parts = send_parts(source, (STEPS - 1) % 2)
 
     def flow_of(field):
         density, momentum = moments(field)
@@ -636,7 +726,12 @@
 
     lax.fori_loop(0, ni, expand, 0, unroll=2)
     lax.fori_loop(1, X - 1, last, 0)
-    finish(copies, source, STEPS - 1)
+    for copy in planes(source, STEPS - 1):
+        copy.wait()
+    for side in (lead, follow):
+        receive_side(source, STEPS - 1, side)
+    for part in parts:
+        part.wait()
     for x in (0, X - 1):
         last(x, 0)
     for side in range(2):
@@ -842,6 +937,7 @@
             pltpu.VMEM((COUNT, X + 2, padded, NZ), f32),
             pltpu.VMEM((2, 2, COUNT, X + 2 * ROWS, NZ), f32),
             pltpu.VMEM((2, CROSS, X + 2 * ROWS, NZ), f32),
+            pltpu.VMEM((2, CROSS, X, NZ), f32),
             pltpu.VMEM((2, 2, CROSS, X + 2 * ROWS, NZ), f32),
             pltpu.VMEM((2, CROSS, X, NZ), jnp.int16),
             pltpu.VMEM((2, 2, CROSS, X, NZ), jnp.int16),

time: 42.1 us -> 41.7 us (level)
  no operation moved by 1% of the time
where the time goes in v4:
time: 41.7 us; the launch traced here: 41.5 us
  Pallas kernels  40.3 us (97%)
  between operations  1.28 us (3%)
    pallas_call x1, Pallas kernels, on_device(): pl.pallas_call(functools.partial(kernel, sizes), out_shape=(pltpu.VMEM(po...  37.9 us
    pallas_call x1, Pallas kernels, on_device(): pl.pallas_call(functools.partial(put_out, pieces), out_shape=tuple((jax.S...  2.38 us

profile of v4, /device:TPU:0, one launch (start us, length us, event | category | flops | bytes accessed | tf_op | source)
XLA Modules:
  0.0 41.5 jit_solution(11868809011179501005)
XLA Ops:
  1.3 37.9 %shard_map.58 = (f32[19,32,16,128]{3,2,1,0:T(8,128)S(1)}, bf16[32,16,128]{2,1,0:T(8,128)(2,1)S(1)}, f32[1,4,32,128]{3,2,1,0:T(8,128)S(1)}) custom-call(f32[19,32,16,128]{3,2,1,0:T(8,128)} %f_hbm.1, f32[5,1,8]{2,1,0:T(1,128)} %bitcast.1, s32[1]{0:T(128)S(6)} %copy.6.direct_hbm), custom_call_target="tpu_custom_call" | custom-call | tf_op jit(solution)/shard_map/pallas_call | solution.py:918
  39.2 2.4 %shard_map.59 = (f32[19,32,16,128]{3,2,1,0:T(8,128)}, bf16[32,16,128]{2,1,0:T(8,128)(2,1)}, f32[1,4,32,128]{3,2,1,0:T(8,128)}) custom-call(f32[19,32,16,128]{3,2,1,0:T(8,128)S(1)} %get-tuple-element.6.F, bf16[32,16,128]{2,1,0:T(8,128)(2,1)S(1)} %get-tuple-element.7.vort, f32[1,4,32,128]{3,2,1,0:T(8,128)S(1)} %get-tuple-element.8.img), custom_call_target="tpu_custom_call" | custom-call | tf_op jit(solution)/shard_map/pallas_call | solution.py:973

commit v5 on v4

--- a/solution.py
+++ b/solution.py
@@ -54,7 +54,7 @@
 ROWS = 8
 CODED = 16
 STEP = 16384.0
-AHEAD = 4
+AHEAD = 5
 PIECE = 65535.0
 PART_UNITS = ((32768.0, 5.0 / 6.0), (65536.0, 0.0), (65536.0, 0.0))
 
@@ -767,7 +767,7 @@
         G[x] = jnp.exp2(-(level * level))
         return carry
 
-    lax.fori_loop(0, X, spin, 0, unroll=4)
+    lax.fori_loop(0, X, spin, 0, unroll=8)
 
     owner = i // ratio
     mine = d * ratio + lax.rem(i, ratio)
@@ -820,7 +820,7 @@
 
         zero = jnp.zeros((ROWS, NZ), jnp.float32)
         start = (zero, jnp.ones((ROWS, NZ), jnp.float32), zero, zero, zero) * halves
-        state = lax.fori_loop(0, X, along, start, unroll=2)
+        state = lax.fori_loop(0, X, along, start, unroll=8)
         parts = []
         for h in range(halves):
             signed, seen, *colors = state[5 * h : 5 * h + 5]

time: 41.7 us -> 40.9 us (0.981)
  Pallas kernels: 40.3 us -> 39.4 us
    pallas_call x1, Pallas kernels: 37.9 us -> 37 us  [on_device(): pl.pallas_call(functools.partial(kernel, sizes), out_shape=(pltpu.VMEM(po...]
where the time goes in v5:
time: 40.9 us; the launch traced here: 40.7 us
  Pallas kernels  39.4 us (96%)
  between operations  1.28 us (3%)
    pallas_call x1, Pallas kernels, on_device(): pl.pallas_call(functools.partial(kernel, sizes), out_shape=(pltpu.VMEM(po...  37 us
    pallas_call x1, Pallas kernels, on_device(): pl.pallas_call(functools.partial(put_out, pieces), out_shape=tuple((jax.S...  2.38 us

profile of v5, /device:TPU:0, one launch (start us, length us, event | category | flops | bytes accessed | tf_op | source)
XLA Modules:
  0.0 40.7 jit_solution(16597506341420423292)
XLA Ops:
  1.3 37.0 %shard_map.58 = (f32[19,32,16,128]{3,2,1,0:T(8,128)S(1)}, bf16[32,16,128]{2,1,0:T(8,128)(2,1)S(1)}, f32[1,4,32,128]{3,2,1,0:T(8,128)S(1)}) custom-call(f32[19,32,16,128]{3,2,1,0:T(8,128)} %f_hbm.1, f32[5,1,8]{2,1,0:T(1,128)} %bitcast.1, s32[1]{0:T(128)S(6)} %copy.6.direct_hbm), custom_call_target="tpu_custom_call" | custom-call | tf_op jit(solution)/shard_map/pallas_call | solution.py:918
  38.3 2.4 %shard_map.59 = (f32[19,32,16,128]{3,2,1,0:T(8,128)}, bf16[32,16,128]{2,1,0:T(8,128)(2,1)}, f32[1,4,32,128]{3,2,1,0:T(8,128)}) custom-call(f32[19,32,16,128]{3,2,1,0:T(8,128)S(1)} %get-tuple-element.6.F, bf16[32,16,128]{2,1,0:T(8,128)(2,1)S(1)} %get-tuple-element.7.vort, f32[1,4,32,128]{3,2,1,0:T(8,128)S(1)} %get-tuple-element.8.img), custom_call_target="tpu_custom_call" | custom-call | tf_op jit(solution)/shard_map/pallas_call | solution.py:973

commit v6 on v5

--- a/solution.py
+++ b/solution.py
@@ -690,6 +690,12 @@
             fill_rows(target, turn % 2)
         for copy in planes(target, turn):
             copy.start()
+        if turn == STEPS - 1:
+            for x in (1, X - 2):
+                inward_rows(target, x)
+            for copy in shares:
+                copy.wait()
+            parts = send_parts(target, turn % 2)
 
         def settle(x, carry, target=target):
             inward_rows(target, x)
@@ -697,10 +703,6 @@
 
         lax.fori_loop(1, X - 1, settle, 0)
         source, target = target, source
-
-    for copy in shares:
-        copy.wait()
-    parts = send_parts(source, (STEPS - 1) % 2)
 
     def flow_of(field):
         density, momentum = moments(field)
@@ -728,12 +730,12 @@
     lax.fori_loop(1, X - 1, last, 0)
     for copy in planes(source, STEPS - 1):
         copy.wait()
+    for x in (0, X - 1):
+        last(x, 0)
     for side in (lead, follow):
         receive_side(source, STEPS - 1, side)
     for part in parts:
         part.wait()
-    for x in (0, X - 1):
-        last(x, 0)
     for side in range(2):
         row = edge_rows[side]
         for x in range(0, X, ROWS):

time: 40.9 us -> 40.7 us (level)
  no operation moved by 1% of the time
where the time goes in v6:
time: 40.7 us; the launch traced here: 40.6 us
  Pallas kernels  39.3 us (97%)
  between operations  1.28 us (3%)
    pallas_call x1, Pallas kernels, on_device(): pl.pallas_call(functools.partial(kernel, sizes), out_shape=(pltpu.VMEM(po...  36.9 us
    pallas_call x1, Pallas kernels, on_device(): pl.pallas_call(functools.partial(put_out, pieces), out_shape=tuple((jax.S...  2.38 us

profile of v6, /device:TPU:0, one launch (start us, length us, event | category | flops | bytes accessed | tf_op | source)
XLA Modules:
  0.0 40.6 jit_solution(17088271536161019438)
XLA Ops:
  1.3 36.9 %shard_map.58 = (f32[19,32,16,128]{3,2,1,0:T(8,128)S(1)}, bf16[32,16,128]{2,1,0:T(8,128)(2,1)S(1)}, f32[1,4,32,128]{3,2,1,0:T(8,128)S(1)}) custom-call(f32[19,32,16,128]{3,2,1,0:T(8,128)} %f_hbm.1, f32[5,1,8]{2,1,0:T(1,128)} %bitcast.1, s32[1]{0:T(128)S(6)} %copy.6.direct_hbm), custom_call_target="tpu_custom_call" | custom-call | tf_op jit(solution)/shard_map/pallas_call | solution.py:920
  38.2 2.4 %shard_map.59 = (f32[19,32,16,128]{3,2,1,0:T(8,128)}, bf16[32,16,128]{2,1,0:T(8,128)(2,1)}, f32[1,4,32,128]{3,2,1,0:T(8,128)}) custom-call(f32[19,32,16,128]{3,2,1,0:T(8,128)S(1)} %get-tuple-element.6.F, bf16[32,16,128]{2,1,0:T(8,128)(2,1)S(1)} %get-tuple-element.7.vort, f32[1,4,32,128]{3,2,1,0:T(8,128)S(1)} %get-tuple-element.8.img), custom_call_target="tpu_custom_call" | custom-call | tf_op jit(solution)/shard_map/pallas_call | solution.py:975

commit v7 on v6

--- a/solution.py
+++ b/solution.py
@@ -727,7 +727,7 @@
         return carry
 
     lax.fori_loop(0, ni, expand, 0, unroll=2)
-    lax.fori_loop(1, X - 1, last, 0)
+    lax.fori_loop(1, X - 1, last, 0, unroll=2)
     for copy in planes(source, STEPS - 1):
         copy.wait()
     for x in (0, X - 1):

time: 40.7 us -> 40.7 us (level)
  no operation moved by 1% of the time
where the time goes in v7:
time: 40.7 us; the launch traced here: 40.6 us
  Pallas kernels  39.3 us (97%)
  between operations  1.28 us (3%)
    pallas_call x1, Pallas kernels, on_device(): pl.pallas_call(functools.partial(kernel, sizes), out_shape=(pltpu.VMEM(po...  36.9 us
    pallas_call x1, Pallas kernels, on_device(): pl.pallas_call(functools.partial(put_out, pieces), out_shape=tuple((jax.S...  2.38 us

profile of v7, /device:TPU:0, one launch (start us, length us, event | category | flops | bytes accessed | tf_op | source)
XLA Modules:
  0.0 40.6 jit_solution(18299520074607261530)
XLA Ops:
  1.3 36.9 %shard_map.58 = (f32[19,32,16,128]{3,2,1,0:T(8,128)S(1)}, bf16[32,16,128]{2,1,0:T(8,128)(2,1)S(1)}, f32[1,4,32,128]{3,2,1,0:T(8,128)S(1)}) custom-call(f32[19,32,16,128]{3,2,1,0:T(8,128)} %f_hbm.1, f32[5,1,8]{2,1,0:T(1,128)} %bitcast.1, s32[1]{0:T(128)S(6)} %copy.6.direct_hbm), custom_call_target="tpu_custom_call" | custom-call | tf_op jit(solution)/shard_map/pallas_call | solution.py:920
  38.2 2.4 %shard_map.59 = (f32[19,32,16,128]{3,2,1,0:T(8,128)}, bf16[32,16,128]{2,1,0:T(8,128)(2,1)}, f32[1,4,32,128]{3,2,1,0:T(8,128)}) custom-call(f32[19,32,16,128]{3,2,1,0:T(8,128)S(1)} %get-tuple-element.6.F, bf16[32,16,128]{2,1,0:T(8,128)(2,1)S(1)} %get-tuple-element.7.vort, f32[1,4,32,128]{3,2,1,0:T(8,128)S(1)} %get-tuple-element.8.img), custom_call_target="tpu_custom_call" | custom-call | tf_op jit(solution)/shard_map/pallas_call | solution.py:975
